TPU v7x, 32 devices: a whole 2x2x4 slice. The times are simulated.
32 devices in a mesh: groups: 2 (over x), wide: 16 (over z, y, core).
Axes of the slice: x: 2, y: 2, z: 4, core: 2. Of those that a mesh axis runs over, the one named last changes fastest.
Arguments:
- queries: bfloat16 [4096, 512], P(('groups', 'wide')), parts along dimension 0, may hold values from -200 to 200, as said below
- tree_kv: bfloat16 [2, 4096, 128], P(None, ('groups', 'wide')), parts along dimension 1, may hold values from -7 to 7, as said below
- kv_cache: bfloat16 [2, 512, 32, 128], P(None, ('groups', 'wide')), parts along dimension 1, may hold values from -6 to 6, as said below
- block_table: int32 [128, 4], P(('groups', 'wide')), parts along dimension 0, may hold values from 0 to 15, as said below
- cache_lengths: int32 [32, 4], P(('groups', 'wide')), parts along dimension 0, may hold values from 1 to 128, as said below
- parents: int32 [128, 32], P(('groups', 'wide')), parts along dimension 0, may hold values from -1 to 30, as said below
- w_out: bfloat16 [8192, 2048], P('wide'), may hold values from -0.375 to 0.375, as said below
- w_gate: bfloat16 [16, 2048, 768], P('wide'), may hold values from -0.125 to 0.125
- w_up: bfloat16 [16, 2048, 768], P('wide'), may hold values from -0.125 to 0.125
- w_down: bfloat16 [16, 768, 2048], P('wide'), may hold values from -0.4375 to 0.4375
- expert_ids: int32 [512, 8], P(('groups', 'wide')), parts along dimension 0, may hold values from 0 to 15, as said below
- gate_weights: float32 [512, 8], P(('groups', 'wide')), parts along dimension 0, may hold values from 0.05 to 0.5
Outputs:
- mixed: bfloat16 [512, 2048], P(('groups', 'wide')), parts along dimension 0
There are 2 independent parts, one for each index of `groups`. A program takes and returns all parts, laid end to end along the dimension named above; an argument that names none is the same for every part. Nothing has to cross between parts.
Inputs may be any that keep to these rules, and one draw needn't show every extreme that they name: `queries`: its hidden draw may carry large entries. `tree_kv`: blocks of one group whose slices use the same key head are equal. `kv_cache`: pools of one group whose slices use the same key head are equal. `block_table`: each device's rows list every page of its pool once; blocks t * 2 + g are equal for all t. `cache_lengths`: rows t * 2 + g are equal for all t; every row holds one length 128 and one length 1. `parents`: node i of a tree has a parent before it; node 0 is the root with parent -1; blocks t * 2 + g are equal for all t. `w_out`: blocks of one head slice are equal. `expert_ids`: each row lists 8 different experts. Within the rows of one device no expert is listed by more than 10 rows; in every draw one expert is listed by exactly 10 rows of every device.
All inputs are finite; a program needn't handle non-finite values.
Results may differ from a plain program's by a relative error of at most 0.0083.
Values may be sent and summed in bfloat16 or wider, within the bound.
A program may use at most 64 MiB of HBM per device.

v0:
```python
import functools

import jax
import jax.numpy as jnp
from jax import lax
from jax.experimental import pallas as pl
from jax.experimental.pallas import tpu as pltpu
from jax.sharding import PartitionSpec as P

ATT_TP = 8
CHUNKS = 4
PERIOD = 2
TILE = 256
LANES = 128
MESH = pl.DeviceIdType.MESH


def spread(weights):
    offsets = [0]
    for weight in weights:
        offsets += [offset + weight for offset in offsets]
    return offsets


def swap_low(place):
    low, high = place // 2 % 2, place // 4 % 2
    return place - 2 * low - 4 * high + 4 * low + 2 * high


def swapped(bits, first, second):
    trade = {first: second, second: first}
    return [trade.get(bit, bit) for bit in bits]


def layer_kernel(
    count,
    block_table,
    cache_lengths,
    queries_in,
    tree_in,
    cache_in,
    parents,
    w_out_in,
    w_gate_in,
    w_up_in,
    w_down_in,
    expert_ids,
    gate_weights,
    out,
    queries,
    tree,
    cache,
    w_out,
    w_gate,
    w_up,
    w_down,
    attended,
    partial,
    hidden,
    routing,
    gate_sum,
    up_sum,
    activated,
    produced,
    send_one,
    recv_one,
    send_two,
    recv_two,
    load_sem,
    one_send_sem,
    one_recv_sem,
    all_send_sem,
    all_recv_sem,
    route_send_sem,
    route_recv_sem,
    two_send_sem,
    two_recv_sem,
):
    me = lax.axis_index("wide")
    bit_count = count.bit_length() - 1
    slice_shift = bit_count - (ATT_TP.bit_length() - 1)
    mine = [(me // (1 << bit)) % 2 for bit in range(bit_count)]
    partner = [me + (1 - 2 * mine[bit]) * (1 << bit) for bit in range(bit_count)]

    barrier = pltpu.get_barrier_semaphore()
    for bit in range(bit_count):
        pl.semaphore_signal(
            barrier, inc=1, device_id={"wide": partner[bit]}, device_id_type=MESH
        )

    loads = []
    for number, (source, target) in enumerate(
        (
            (queries_in, queries),
            (tree_in, tree),
            (cache_in, cache),
            (w_out_in, w_out),
            (w_gate_in.at[0], w_gate),
            (w_up_in.at[0], w_up),
            (w_down_in.at[0], w_down),
        )
    ):
        copy = pltpu.make_async_copy(source, target, load_sem.at[number])
        if number < 4:
            copy.start()
        loads.append(copy)

    rows = out.shape[0]
    ids = expert_ids[...].T
    weights_of = gate_weights[...].T
    lane_ids = lax.broadcasted_iota(jnp.int32, (rows, routing.shape[2]), 1)
    row_weight = jnp.zeros((rows, routing.shape[2]), jnp.float32)
    for k in range(expert_ids.shape[0]):
        row_weight += jnp.where(
            ids[:, k : k + 1] == lane_ids, weights_of[:, k : k + 1], 0.0
        )
    routing_rows = row_weight

    seq_count, node_count = parents.shape
    head_dim = tree.shape[2]
    head_count = queries.shape[1] // head_dim
    page_count = block_table.shape[1]
    node_rows = lax.broadcasted_iota(jnp.int32, (node_count, node_count), 0)
    node_cols = lax.broadcasted_iota(jnp.int32, (node_count, node_count), 1)
    closures = []
    for seq in range(seq_count):
        linked = ((parents[seq : seq + 1, :] == node_rows) | (node_rows == node_cols)).astype(
            jnp.float32
        )
        closures.append(linked)
    for repeat in range(max(node_count - 1, 1).bit_length()):
        narrow = [linked.astype(jnp.bfloat16) for linked in closures]
        closures = [
            jnp.minimum(jnp.dot(linked, linked, preferred_element_type=jnp.float32), 1.0)
            for linked in narrow
        ]

    for copy in loads[:3]:
        copy.wait()
    cached = page_count * cache.shape[2]
    positions = lax.broadcasted_iota(jnp.int32, (head_count * node_count, cached), 1)
    across = (((1,), (1,)), ((), ()))
    for seq in range(seq_count):
        first = seq * node_count
        last = first + node_count
        stacked = jnp.concatenate(
            [
                queries[first:last, head * head_dim : (head + 1) * head_dim]
                for head in range(head_count)
            ],
            axis=0,
        )
        pages = [block_table[seq, page] for page in range(page_count)]
        keys = jnp.concatenate([cache[0, page] for page in pages], axis=0)
        values = jnp.concatenate([cache[1, page] for page in pages], axis=0)
        scale = head_dim ** (-0.5)
        cache_scores = (
            lax.dot_general(stacked, keys, across, preferred_element_type=jnp.float32) * scale
        )
        tree_scores = (
            lax.dot_general(
                stacked, tree[0, first:last], across, preferred_element_type=jnp.float32
            )
            * scale
        )
        seen = jnp.concatenate([closures[seq].T] * head_count, axis=0) > 0.5
        cache_scores = jnp.where(positions < cache_lengths[0, seq], cache_scores, -jnp.inf)
        tree_scores = jnp.where(seen, tree_scores, -jnp.inf)
        highest = jnp.maximum(
            jnp.max(cache_scores, axis=1, keepdims=True),
            jnp.max(tree_scores, axis=1, keepdims=True),
        )
        cache_probs = jnp.exp(cache_scores - highest)
        tree_probs = jnp.exp(tree_scores - highest)
        denominator = jnp.sum(cache_probs, axis=1, keepdims=True) + jnp.sum(
            tree_probs, axis=1, keepdims=True
        )
        blended = jnp.dot(
            cache_probs.astype(jnp.bfloat16), values, preferred_element_type=jnp.float32
        ) + jnp.dot(
            tree_probs.astype(jnp.bfloat16),
            tree[1, first:last],
            preferred_element_type=jnp.float32,
        )
        blended = (blended / denominator).astype(jnp.bfloat16)
        for head in range(head_count):
            attended[first:last, head * head_dim : (head + 1) * head_dim] = blended[
                head * node_count : (head + 1) * node_count
            ]

    started = []

    def send(source, target, send_sem, recv_sem, bit):
        copy = pltpu.make_async_remote_copy(
            src_ref=source,
            dst_ref=target,
            send_sem=send_sem,
            recv_sem=recv_sem,
            device_id={"wide": partner[bit]},
            device_id_type=MESH,
        )
        copy.start()
        started.append(copy)
        return copy

    width = w_out.shape[1] // CHUNKS
    spans = [slice(chunk * width, (chunk + 1) * width) for chunk in range(CHUNKS)]

    class Halving:
        def __init__(self, total, out_buffer, in_buffer, send_sems, recv_sems, weights, orders):
            self.total = total
            self.out_buffer = out_buffer
            self.in_buffer = in_buffer
            self.send_sems = send_sems
            self.recv_sems = recv_sems
            self.weights = weights
            self.orders = orders
            self.steps = len(orders[0])
            self.copies = {}
            self.extra = []

        def places(self, chunk, step):
            order = self.orders[int(chunk % PERIOD == PERIOD - 1)]
            base = 0
            for bit in order[:step]:
                base = base + mine[bit] * self.weights[bit]
            bit = order[step]
            offsets = spread([self.weights[other] for other in order[step + 1 :]] + self.extra)
            weight = self.weights[bit]
            kept = [base + mine[bit] * weight + offset for offset in offsets]
            sent = [base + (1 - mine[bit]) * weight + offset for offset in offsets]
            first = sum(
                (1 << (self.steps - 1 - past)) << len(self.extra) for past in range(step)
            )
            return bit, kept, sent, first

        def start(self, chunk, step):
            self.fill(chunk, step)
            self.launch(chunk, step)

        def fill(self, chunk, step):
            bit, kept, sent, first = self.places(chunk, step)
            for number, place in enumerate(sent):
                self.out_buffer[chunk, first + number] = self.total[
                    place, :, spans[chunk]
                ].astype(jnp.bfloat16)

        def launch(self, chunk, step):
            bit, kept, sent, first = self.places(chunk, step)
            region = pl.ds(first, len(sent))
            self.copies[chunk, step] = send(
                self.out_buffer.at[chunk, region],
                self.in_buffer.at[chunk, region],
                self.send_sems.at[chunk, step],
                self.recv_sems.at[chunk, step],
                bit,
            )

        def finish(self, chunk, step):
            bit, kept, sent, first = self.places(chunk, step)
            self.copies[chunk, step].wait_recv()
            for number, place in enumerate(kept):
                self.total[place, :, spans[chunk]] += self.in_buffer[
                    chunk, first + number
                ].astype(jnp.float32)

    class Doubling:
        def __init__(self, buffer, send_sems, recv_sems, order):
            self.buffer = buffer
            self.send_sems = send_sems
            self.recv_sems = recv_sems
            self.order = order
            self.copies = {}

        def base(self, step):
            place = 0
            for later in range(step, bit_count):
                place = place + mine[self.order[later]] * (1 << later)
            return place

        def start(self, step):
            view = self.buffer.at[pl.ds(self.base(step), 1 << step)]
            self.copies[step] = send(
                view, view, self.send_sems.at[step], self.recv_sems.at[step], self.order[step]
            )

        def finish(self, step):
            self.copies[step].wait_recv()

    all_bits = list(range(bit_count))
    slice_bits = all_bits[slice_shift:]
    trade = (bit_count - 2, bit_count - 3)
    far_bit = slice_bits[-1]
    slice_weights = {bit: 1 << (bit - slice_shift) for bit in slice_bits}
    place_weights = {bit: 1 << (bit_count - 1 - bit) for bit in all_bits}
    first_sum = Halving(
        partial, send_one, recv_one, one_send_sem, one_recv_sem, slice_weights,
        (slice_bits[:-1], swapped(slice_bits[:-1], *trade)),
    )
    first_sum.extra = [slice_weights[far_bit]]
    second_orders = (all_bits, swapped(all_bits, *trade))
    second_sum = Halving(
        produced, send_two, recv_two, two_send_sem, two_recv_sem, place_weights, second_orders
    )
    gathers = [
        Doubling(
            hidden.at[chunk], all_send_sem.at[chunk], all_recv_sem.at[chunk],
            second_orders[int(chunk % PERIOD == PERIOD - 1)][::-1],
        )
        for chunk in range(CHUNKS)
    ]
    route = Doubling(routing, route_send_sem, route_recv_sem, all_bits[::-1])
    my_place = route.base(0)
    routing[my_place] = routing_rows

    last_step = len(slice_bits) - 1
    far_first = (1 << last_step) * 2 - 2

    def far_places():
        base = 0
        for bit in slice_bits[:-1]:
            base = base + mine[bit] * slice_weights[bit]
        return [base, base + slice_weights[far_bit]]

    far_copies = {}

    def far_start(chunk):
        for number, place in enumerate(far_places()):
            send_one[chunk, far_first + number] = partial[place, :, spans[chunk]].astype(
                jnp.bfloat16
            )
        region = pl.ds(far_first, 2)
        far_copies[chunk] = send(
            send_one.at[chunk, region], recv_one.at[chunk, region],
            one_send_sem.at[chunk, last_step], one_recv_sem.at[chunk, last_step], far_bit,
        )

    def far_finish(chunk):
        far_copies[chunk].wait_recv()
        base = gathers[chunk].base(1)
        for number, place in enumerate(far_places()):
            hidden[chunk, base + number] = (
                partial[place, :, spans[chunk]]
                + recv_one[chunk, far_first + number].astype(jnp.float32)
            ).astype(jnp.bfloat16)

    loads[3].wait()
    for copy in loads[4:]:
        copy.start()
    for chunk in range(CHUNKS):
        projected = jnp.dot(
            attended[...], w_out[:, spans[chunk]], preferred_element_type=jnp.float32
        )
        partial[:, :, spans[chunk]] = projected.reshape(partial.shape[0], rows, width)
        first_sum.fill(chunk, 0)
    pl.semaphore_wait(barrier, bit_count)
    for chunk in range(CHUNKS):
        first_sum.launch(chunk, 0)
    route.start(0)
    for step in range(last_step):
        for chunk in range(CHUNKS):
            first_sum.finish(chunk, step)
            if step + 1 < last_step:
                first_sum.start(chunk, step + 1)
            else:
                far_start(chunk)
    route.finish(0)
    route.start(1)
    for chunk in range(CHUNKS):
        far_finish(chunk)
        gathers[chunk].start(1)
    for step in range(1, bit_count):
        for chunk in range(CHUNKS):
            if step + 1 < bit_count:
                gathers[chunk].finish(step)
                gathers[chunk].start(step + 1)
        route.finish(step)
        if step + 1 < bit_count:
            route.start(step + 1)
    loads[4].wait()
    loads[5].wait()

    blocks = TILE // rows if count * rows > TILE else count
    groups = count // blocks
    tile_rows = blocks * rows
    hidden_width = w_gate.shape[1]
    cuts = [
        slice(start, min(start + TILE, hidden_width)) for start in range(0, hidden_width, TILE)
    ]

    def over_groups(step):
        if groups == 1:
            step(0)
        else:
            pl.loop(0, groups)(step)

    for chunk in range(CHUNKS):
        gathers[chunk].finish(bit_count - 1)

        def accumulate(group, chunk=chunk):
            taken = hidden[chunk, pl.ds(group * blocks, blocks)]
            if chunk % PERIOD == PERIOD - 1:
                order = [swap_low(block) for block in range(blocks)]
                taken = jnp.concatenate([taken[block : block + 1] for block in order], axis=0)
            taken = taken.reshape(tile_rows, width)
            for cut in cuts:
                for sums, weights in ((gate_sum, w_gate), (up_sum, w_up)):
                    part = jnp.dot(
                        taken, weights[spans[chunk], cut], preferred_element_type=jnp.float32
                    )
                    if chunk == 0:
                        sums[group, :, cut] = part
                    else:
                        sums[group, :, cut] += part

        over_groups(accumulate)

    def activate(group):
        for cut in cuts:
            gate = gate_sum[group, :, cut]
            activated[group, :, cut] = (
                gate / (1.0 + jnp.exp(-gate)) * up_sum[group, :, cut]
            ).astype(jnp.bfloat16)

    over_groups(activate)
    loads[6].wait()
    for chunk in range(CHUNKS):

        def down(group, chunk=chunk):
            made = jnp.dot(
                activated[group], w_down[:, spans[chunk]], preferred_element_type=jnp.float32
            )
            table = routing[pl.ds(group * blocks, blocks)].reshape(tile_rows, routing.shape[2])
            experts = lax.broadcasted_iota(jnp.int32, table.shape, 1)
            weight = jnp.sum(jnp.where(experts == me, table, 0.0), axis=1, keepdims=True)
            produced[pl.ds(group * blocks, blocks), :, spans[chunk]] = (made * weight).reshape(
                blocks, rows, width
            )

        over_groups(down)
        second_sum.start(chunk, 0)
    for step in range(second_sum.steps):
        for chunk in range(CHUNKS):
            second_sum.finish(chunk, step)
            if step + 1 < second_sum.steps:
                second_sum.start(chunk, step + 1)
            else:
                out[:, spans[chunk]] = produced[my_place, :, spans[chunk]].astype(jnp.bfloat16)
    for copy in started:
        copy.wait_send()


def body(
    queries,
    tree_kv,
    kv_cache,
    block_table,
    cache_lengths,
    parents,
    w_out,
    w_gate,
    w_up,
    w_down,
    expert_ids,
    gate_weights,
):
    count = lax.axis_size("wide")
    rows = expert_ids.shape[0]
    features = w_out.shape[1]
    hidden_width = w_gate.shape[2]
    bit_count = count.bit_length() - 1
    slice_steps = ATT_TP.bit_length() - 1
    width = features // CHUNKS
    lanes = -(-count // LANES) * LANES
    blocks = TILE // rows if count * rows > TILE else count
    groups = count // blocks
    tile_rows = blocks * rows
    hbm = pl.BlockSpec(memory_space=pl.ANY)
    vmem = pl.BlockSpec(memory_space=pltpu.VMEM)
    smem = pl.BlockSpec(memory_space=pltpu.SMEM)
    dma = pltpu.SemaphoreType.DMA
    return pl.pallas_call(
        functools.partial(layer_kernel, count),
        out_shape=jax.ShapeDtypeStruct((rows, features), jnp.bfloat16),
        in_specs=[smem, smem, hbm, hbm, hbm, vmem, hbm, hbm, hbm, hbm, vmem, vmem],
        out_specs=vmem,
        scratch_shapes=[
            pltpu.VMEM(queries.shape, queries.dtype),
            pltpu.VMEM(tree_kv.shape, tree_kv.dtype),
            pltpu.VMEM(kv_cache.shape, kv_cache.dtype),
            pltpu.VMEM(w_out.shape, w_out.dtype),
            pltpu.VMEM(w_gate.shape[1:], w_gate.dtype),
            pltpu.VMEM(w_up.shape[1:], w_up.dtype),
            pltpu.VMEM(w_down.shape[1:], w_down.dtype),
            pltpu.VMEM(queries.shape, jnp.bfloat16),
            pltpu.VMEM((ATT_TP, rows, features), jnp.float32),
            pltpu.VMEM((CHUNKS, count, rows, width), jnp.bfloat16),
            pltpu.VMEM((count, rows, lanes), jnp.float32),
            pltpu.VMEM((groups, tile_rows, hidden_width), jnp.float32),
            pltpu.VMEM((groups, tile_rows, hidden_width), jnp.float32),
            pltpu.VMEM((groups, tile_rows, hidden_width), jnp.bfloat16),
            pltpu.VMEM((count, rows, features), jnp.float32),
            pltpu.VMEM((CHUNKS, ATT_TP, rows, width), jnp.bfloat16),
            pltpu.VMEM((CHUNKS, ATT_TP, rows, width), jnp.bfloat16),
            pltpu.VMEM((CHUNKS, count - 1, rows, width), jnp.bfloat16),
            pltpu.VMEM((CHUNKS, count - 1, rows, width), jnp.bfloat16),
            dma((7,)),
            dma((CHUNKS, slice_steps)),
            dma((CHUNKS, slice_steps)),
            dma((CHUNKS, bit_count)),
            dma((CHUNKS, bit_count)),
            dma((bit_count,)),
            dma((bit_count,)),
            dma((CHUNKS, bit_count)),
            dma((CHUNKS, bit_count)),
        ],
        compiler_params=pltpu.CompilerParams(
            collective_id=0, has_side_effects=True, vmem_limit_bytes=60 << 20
        ),
    )(
        block_table,
        cache_lengths,
        queries,
        tree_kv,
        kv_cache,
        parents,
        w_out,
        w_gate,
        w_up,
        w_down,
        expert_ids.T,
        gate_weights.T,
    )


def solution(mesh):
    placed = (
        P(("groups", "wide"), None),
        P(None, ("groups", "wide"), None),
        P(None, ("groups", "wide"), None, None),
        P(("groups", "wide"), None),
        P(("groups", "wide"), None),
        P(("groups", "wide"), None),
        P("wide", None),
        P("wide", None, None),
        P("wide", None, None),
        P("wide", None, None),
        P(("groups", "wide"), None),
        P(("groups", "wide"), None),
    )
    return jax.shard_map(
        body, mesh=mesh, in_specs=placed, out_specs=P(("groups", "wide"), None), check_vma=False
    )
```

profile of v0, /device:TPU:0, one launch (start us, length us, event | category | flops | bytes accessed | tf_op | source)
XLA Modules:
  0.0 44.2 jit_solution(8181281167751010896)
XLA Ops:
  0.0 42.7 %shard_map.118 = bf16[16,2048]{1,0:T(8,128)(2,1)} custom-call(s32[4,4]{1,0:T(4,128)} %block_table.1, s32[1,4]{1,0:T(1,128)} %cache_lengths.1, bf16[128,512]{1,0:T(8,128)(2,1)} %queries_in.1, bf16[2,128,128]{2,1,0:T(8,128)(2,1)} %tree_in.1, bf16[2,16,32,128]{3,2,1,0:T(8,128)(2,1)} %cache_in.1, s32[4,32]{1,0:T(4,128)} %parents.1, bf16[512,2048]{1,0:T(8,128)(2,1)} %w_out_in.1, ...), custom_call_target="tpu_custom_call" | custom-call | tf_op jit(solution)/shard_map/pallas_call | solution.py:482
  42.7 1.5 %copy.14 = bf16[16,2048]{1,0:T(8,128)(2,1)} copy(bf16[16,2048]{1,0:T(8,128)(2,1)} %shard_map.118) | data formatting | bytes 131072
where the time goes:
time: 44.4 us; the launch traced here: 44.2 us
  Pallas kernels  42.7 us (96%)
  local copies, waits for them, and re-layouts  1.47 us (3%)
    pallas_call x1, Pallas kernels, body(): pl.pallas_call(functools.partial(layer_kernel, count), out_shape=jax.Shap...  42.7 us
    unnamed x1, local copies, waits for them, and re-layouts  1.47 us

commit v1 on v0

v1 whole, which is shorter than its diff:
```python
import functools

import jax
import jax.numpy as jnp
from jax import lax
from jax.experimental import pallas as pl
from jax.experimental.pallas import tpu as pltpu
from jax.sharding import PartitionSpec as P

CHUNKS = 4
TILE = 256
LANES = 128
MESH = pl.DeviceIdType.MESH


def layout(count, slices):
    bits = list(range(count.bit_length() - 1))
    shift = len(bits) - (slices.bit_length() - 1)
    far, near = bits[-1:], bits[shift:-1]
    groups = [tuple(far), tuple(near)]
    low = bits[1:shift]
    while low:
        groups.append(tuple(low[-2:]))
        low = low[:-2]
    if shift > 0:
        groups.append((0,))
    groups = [group for group in groups if group]
    starts = [0]
    for group in groups:
        starts.append(starts[-1] + len(group))
    return groups, starts, shift


def farthest_first(size):
    return sorted(range(1, 1 << size), key=lambda p: (-bin(p).count("1"), p))


def layer_kernel(
    count,
    block_table_in,
    cache_lengths_in,
    queries_in,
    tree_in,
    cache_in,
    parents_in,
    w_out_in,
    w_gate_in,
    w_up_in,
    w_down_in,
    expert_ids_in,
    gate_weights_in,
    out,
    block_table,
    cache_lengths,
    parents,
    expert_ids,
    gate_weights,
    queries,
    tree,
    cache,
    w_out,
    w_gate,
    w_up,
    w_down,
    attended,
    partial,
    hidden,
    routing,
    row_weight,
    gate_sum,
    up_sum,
    activated,
    produced,
    send_one,
    recv_one,
    send_two,
    recv_two,
    load_sem,
    one_send_sem,
    one_recv_sem,
    all_send_sem,
    all_recv_sem,
    route_send_sem,
    route_recv_sem,
    two_send_sem,
    two_recv_sem,
):
    me = lax.axis_index("wide")
    rows = out.shape[0]
    slices = attended.shape[0]
    groups, starts, slice_shift = layout(count, slices)
    bit_count = starts[-1]
    mine = [(me // (1 << bit)) % 2 for bit in range(bit_count)]

    def peer(group, pattern):
        device = me
        for number, bit in enumerate(group):
            if pattern >> number & 1:
                device = device + (1 - 2 * mine[bit]) * (1 << bit)
        return device

    barrier = pltpu.get_barrier_semaphore()
    friends = 0
    for group in groups:
        for pattern in range(1, 1 << len(group)):
            pl.semaphore_signal(
                barrier, inc=1, device_id={"wide": peer(group, pattern)}, device_id_type=MESH
            )
            friends += 1

    loads = []
    for number, (source, target) in enumerate(
        (
            (parents_in, parents),
            (queries_in, queries),
            (tree_in, tree),
            (cache_in, cache),
            (block_table_in, block_table),
            (cache_lengths_in, cache_lengths),
            (expert_ids_in, expert_ids),
            (gate_weights_in, gate_weights),
            (w_out_in, w_out),
            (w_gate_in.at[0], w_gate),
            (w_up_in.at[0], w_up),
            (w_down_in.at[0], w_down),
        )
    ):
        copy = pltpu.make_async_copy(source, target, load_sem.at[number])
        if number < 9:
            copy.start()
        loads.append(copy)

    seq_count, node_count = parents.shape
    head_dim = tree.shape[2]
    head_count = queries.shape[1] // head_dim
    page_count = block_table.shape[1]
    node_rows = lax.broadcasted_iota(jnp.int32, (node_count, node_count), 0)
    node_cols = lax.broadcasted_iota(jnp.int32, (node_count, node_count), 1)
    loads[0].wait()
    closures = []
    for seq in range(seq_count):
        linked = ((parents[seq : seq + 1, :] == node_rows) | (node_rows == node_cols)).astype(
            jnp.float32
        )
        closures.append(linked)
    for repeat in range(max(node_count - 1, 1).bit_length()):
        narrow = [linked.astype(jnp.bfloat16) for linked in closures]
        closures = [
            jnp.minimum(jnp.dot(linked, linked, preferred_element_type=jnp.float32), 1.0)
            for linked in narrow
        ]

    def relative_slice(place):
        index = 0
        for group, start in zip(groups, starts):
            for number, bit in enumerate(group):
                if bit >= slice_shift:
                    fixed = place >> (bit - slice_shift) & 1
                    index = index + (1 - mine[bit] if fixed else mine[bit]) * (
                        1 << (start + number)
                    )
        return index

    for copy in loads[1:6]:
        copy.wait()
    cached = page_count * cache.shape[2]
    positions = lax.broadcasted_iota(jnp.int32, (head_count * node_count, cached), 1)
    across = (((1,), (1,)), ((), ()))
    for seq in range(seq_count):
        first = seq * node_count
        last = first + node_count
        stacked = jnp.concatenate(
            [
                queries[first:last, head * head_dim : (head + 1) * head_dim]
                for head in range(head_count)
            ],
            axis=0,
        )
        pages = [block_table[seq, page] for page in range(page_count)]
        keys = jnp.concatenate([cache[0, page] for page in pages], axis=0)
        values = jnp.concatenate([cache[1, page] for page in pages], axis=0)
        scale = head_dim ** (-0.5)
        cache_scores = (
            lax.dot_general(stacked, keys, across, preferred_element_type=jnp.float32) * scale
        )
        tree_scores = (
            lax.dot_general(
                stacked, tree[0, first:last], across, preferred_element_type=jnp.float32
            )
            * scale
        )
        seen = jnp.concatenate([closures[seq].T] * head_count, axis=0) > 0.5
        cache_scores = jnp.where(positions < cache_lengths[0, seq], cache_scores, -jnp.inf)
        tree_scores = jnp.where(seen, tree_scores, -jnp.inf)
        highest = jnp.maximum(
            jnp.max(cache_scores, axis=1, keepdims=True),
            jnp.max(tree_scores, axis=1, keepdims=True),
        )
        cache_probs = jnp.exp(cache_scores - highest)
        tree_probs = jnp.exp(tree_scores - highest)
        denominator = jnp.sum(cache_probs, axis=1, keepdims=True) + jnp.sum(
            tree_probs, axis=1, keepdims=True
        )
        blended = jnp.dot(
            cache_probs.astype(jnp.bfloat16), values, preferred_element_type=jnp.float32
        ) + jnp.dot(
            tree_probs.astype(jnp.bfloat16),
            tree[1, first:last],
            preferred_element_type=jnp.float32,
        )
        blended = (blended / denominator).astype(jnp.bfloat16)
        for part in range(node_count // rows):
            index = relative_slice((first + part * rows) // rows)
            for head in range(head_count):
                top = head * node_count + part * rows
                attended[index, :, head * head_dim : (head + 1) * head_dim] = blended[
                    top : top + rows
                ]

    started = []

    def send(source, target, send_sem, recv_sem, device):
        copy = pltpu.make_async_remote_copy(
            src_ref=source,
            dst_ref=target,
            send_sem=send_sem,
            recv_sem=recv_sem,
            device_id={"wide": device},
            device_id_type=MESH,
        )
        copy.start()
        started.append(copy)
        return copy

    width = w_out.shape[1] // CHUNKS
    spans = [slice(chunk * width, (chunk + 1) * width) for chunk in range(CHUNKS)]

    class Gather:
        def __init__(self, buffer, send_sems, recv_sems):
            self.buffer = buffer
            self.send_sems = send_sems
            self.recv_sems = recv_sems
            self.copies = {}

        def start(self, step):
            held = 1 << starts[step]
            number = sum((1 << len(group)) - 1 for group in groups[:step])
            copies = []
            for pattern in farthest_first(len(groups[step])):
                slot = number + pattern - 1
                copies.append(
                    send(
                        self.buffer.at[pl.ds(0, held)],
                        self.buffer.at[pl.ds(pattern * held, held)],
                        self.send_sems.at[slot],
                        self.recv_sems.at[slot],
                        peer(groups[step], pattern),
                    )
                )
            self.copies[step] = copies

        def finish(self, step):
            for copy in self.copies[step]:
                copy.wait_recv()

    class Scatter:
        def __init__(self, kept, out_buffer, in_buffer, send_sems, recv_sems, steps):
            self.kept = kept
            self.out_buffer = out_buffer
            self.in_buffer = in_buffer
            self.send_sems = send_sems
            self.recv_sems = recv_sems
            self.steps = steps
            self.copies = {}
            self.first = {}
            self.number = {}
            first = number = 0
            for step in steps:
                self.first[step] = first
                self.number[step] = number
                first += (1 << starts[step + 1]) - (1 << starts[step])
                number += (1 << len(groups[step])) - 1

        def slot(self, step, place):
            return self.first[step] + place - (1 << starts[step])

        def launch(self, chunk, step, pattern):
            held = 1 << starts[step]
            region = pl.ds(self.slot(step, pattern * held), held)
            number = self.number[step] + pattern - 1
            self.copies.setdefault((chunk, step), []).append(
                send(
                    self.out_buffer.at[chunk, region],
                    self.in_buffer.at[chunk, region],
                    self.send_sems.at[chunk, number],
                    self.recv_sems.at[chunk, number],
                    peer(groups[step], pattern),
                )
            )

        def start(self, chunk, step, value):
            held = 1 << starts[step]
            for pattern in farthest_first(len(groups[step])):
                for place in range(pattern * held, (pattern + 1) * held):
                    self.out_buffer[chunk, self.slot(step, place)] = value(place).astype(
                        jnp.bfloat16
                    )
                self.launch(chunk, step, pattern)
            for place in range(held):
                self.kept[place, :, spans[chunk]] = value(place)

        def finish(self, chunk, step):
            for copy in self.copies[chunk, step]:
                copy.wait_recv()

        def value(self, chunk, step, place):
            total = self.kept[place, :, spans[chunk]]
            held = 1 << starts[step]
            for pattern in range(1, 1 << len(groups[step])):
                total = total + self.in_buffer[
                    chunk, self.slot(step, pattern * held + place)
                ].astype(jnp.float32)
            return total

    far_step, near_step, last_step = 0, 1, len(groups) - 1
    first_sum = Scatter(partial, send_one, recv_one, one_send_sem, one_recv_sem, [near_step])
    second_sum = Scatter(
        produced, send_two, recv_two, two_send_sem, two_recv_sem,
        list(range(last_step, -1, -1)),
    )
    gathers = [
        Gather(hidden.at[chunk], all_send_sem.at[chunk], all_recv_sem.at[chunk])
        for chunk in range(CHUNKS)
    ]
    route = Gather(routing, route_send_sem, route_recv_sem)

    loads[6].wait()
    loads[7].wait()
    ids = expert_ids[...].T
    weights_of = gate_weights[...].T
    lane_ids = lax.broadcasted_iota(jnp.int32, (rows, routing.shape[2]), 1)
    listed = jnp.zeros((rows, routing.shape[2]), jnp.float32)
    for k in range(expert_ids.shape[0]):
        listed += jnp.where(ids[:, k : k + 1] == lane_ids, weights_of[:, k : k + 1], 0.0)
    routing[0] = listed

    loads[8].wait()
    for copy in loads[9:]:
        copy.start()
    for chunk in range(CHUNKS):
        projected = jnp.dot(
            attended[...].reshape(slices * rows, attended.shape[2]),
            w_out[:, spans[chunk]],
            preferred_element_type=jnp.float32,
        )
        if chunk == 0:
            pl.semaphore_wait(barrier, friends)
        first_sum.start(
            chunk, near_step, lambda place: projected[place * rows : (place + 1) * rows]
        )
    route.start(far_step)

    held = 1 << starts[near_step]
    far_base = (slices - held)
    far_copies = {}
    far_sem = (1 << len(groups[near_step])) - 1
    for chunk in range(CHUNKS):
        first_sum.finish(chunk, near_step)
        for place in range(held):
            value = first_sum.value(chunk, near_step, place)
            partial[place, :, spans[chunk]] = value
            send_one[chunk, far_base + held - 1 - place] = value.astype(jnp.bfloat16)
        region = pl.ds(far_base, held)
        far_copies[chunk] = send(
            send_one.at[chunk, region],
            recv_one.at[chunk, region],
            one_send_sem.at[chunk, far_sem],
            one_recv_sem.at[chunk, far_sem],
            peer(groups[far_step], 1),
        )
    route.finish(far_step)
    route.start(near_step)
    for chunk in range(CHUNKS):
        far_copies[chunk].wait_recv()
        for place in range(held):
            hidden[chunk, place] = (
                partial[place, :, spans[chunk]]
                + recv_one[chunk, far_base + place].astype(jnp.float32)
            ).astype(jnp.bfloat16)
        gathers[chunk].start(near_step)

    for step in range(near_step, last_step):
        route.finish(step)
        route.start(step + 1)
        if step + 1 < last_step:
            for chunk in range(CHUNKS):
                gathers[chunk].finish(step)
                gathers[chunk].start(step + 1)

    hidden_width = w_gate.shape[1]
    tiles, tile_rows = activated.shape[:2]
    tile_blocks = tile_rows // rows
    joined = max(1, min(TILE // tile_rows, tiles))
    cuts = [
        slice(start, min(start + TILE, hidden_width)) for start in range(0, hidden_width, TILE)
    ]

    def over(total, step):
        if total == 1:
            step(0)
        else:
            pl.loop(0, total)(step)

    def accumulate_chunk(chunk):
        def accumulate(group):
            blocks = tile_blocks * joined
            taken = hidden[chunk, pl.ds(group * blocks, blocks)].reshape(
                blocks * rows, width
            )
            for cut in cuts:
                for sums, weights in ((gate_sum, w_gate), (up_sum, w_up)):
                    part = jnp.dot(
                        taken, weights[spans[chunk], cut], preferred_element_type=jnp.float32
                    )
                    for number in range(joined):
                        piece = part[number * tile_rows : (number + 1) * tile_rows]
                        if chunk == 0:
                            sums[group * joined + number, :, cut] = piece
                        else:
                            sums[group * joined + number, :, cut] += piece

        over(tiles // joined, accumulate)

    for chunk in range(CHUNKS):
        if last_step > near_step:
            gathers[chunk].finish(last_step - 1)
            gathers[chunk].start(last_step)
        if chunk == 0:
            loads[9].wait()
            loads[10].wait()
        else:
            gathers[chunk - 1].finish(last_step)
            accumulate_chunk(chunk - 1)
    route.finish(last_step)

    def weigh(tile):
        table = routing[pl.ds(tile * tile_blocks, tile_blocks)].reshape(
            tile_rows, routing.shape[2]
        )
        experts = lax.broadcasted_iota(jnp.int32, table.shape, 1)
        weight = jnp.sum(jnp.where(experts == me, table, 0.0), axis=1, keepdims=True)
        row_weight[tile] = jnp.broadcast_to(weight, (tile_rows, LANES))

    over(tiles, weigh)
    gathers[CHUNKS - 1].finish(last_step)
    accumulate_chunk(CHUNKS - 1)

    def activate(tile):
        for cut in cuts:
            gate = gate_sum[tile, :, cut]
            activated[tile, :, cut] = (
                gate / (1.0 + jnp.exp(-gate)) * up_sum[tile, :, cut]
            ).astype(jnp.bfloat16)

    over(tiles, activate)
    loads[11].wait()

    def down(chunk, tile):
        made = jnp.dot(
            activated[tile], w_down[:, spans[chunk]], preferred_element_type=jnp.float32
        )
        weight = jnp.concatenate([row_weight[tile]] * (width // LANES), axis=1)
        return (made * weight).reshape(tile_blocks, rows, width)

    half = tiles // 2
    for chunk in range(CHUNKS):

        def give(tile, chunk=chunk):
            first = second_sum.slot(last_step, (1 << starts[last_step])) + tile * tile_blocks
            send_two[chunk, pl.ds(first, tile_blocks)] = down(chunk, half + tile).astype(
                jnp.bfloat16
            )

        over(half, give)
        second_sum.launch(chunk, last_step, 1)
    for chunk in range(CHUNKS):

        def keep(tile, chunk=chunk):
            produced[pl.ds(tile * tile_blocks, tile_blocks), :, spans[chunk]] = down(chunk, tile)

        over(half, keep)
    for step in second_sum.steps:
        for chunk in range(CHUNKS):
            second_sum.finish(chunk, step)
            if step > 0:
                second_sum.start(
                    chunk, step - 1, functools.partial(second_sum.value, chunk, step)
                )
            else:
                out[:, spans[chunk]] = second_sum.value(chunk, step, 0).astype(jnp.bfloat16)
    for copy in started:
        copy.wait_send()


def body(
    queries,
    tree_kv,
    kv_cache,
    block_table,
    cache_lengths,
    parents,
    w_out,
    w_gate,
    w_up,
    w_down,
    expert_ids,
    gate_weights,
):
    count = lax.axis_size("wide")
    rows = expert_ids.shape[0]
    features = w_out.shape[1]
    hidden_width = w_gate.shape[2]
    slices = queries.shape[0] // rows
    groups, starts, slice_shift = layout(count, slices)
    width = features // CHUNKS
    lanes = -(-count // LANES) * LANES
    half_rows = count * rows // 2
    tile_rows = min(TILE, half_rows)
    tiles = count * rows // tile_rows
    links = sum((1 << len(group)) - 1 for group in groups)
    near = (1 << len(groups[1])) - 1
    hbm = pl.BlockSpec(memory_space=pl.ANY)
    vmem = pl.BlockSpec(memory_space=pltpu.VMEM)
    dma = pltpu.SemaphoreType.DMA
    ids, weights_of = expert_ids.T, gate_weights.T
    return pl.pallas_call(
        functools.partial(layer_kernel, count),
        out_shape=pltpu.VMEM((rows, features), jnp.bfloat16),
        in_specs=[hbm] * 12,
        out_specs=vmem,
        scratch_shapes=[
            pltpu.SMEM(block_table.shape, block_table.dtype),
            pltpu.SMEM(cache_lengths.shape, cache_lengths.dtype),
            pltpu.VMEM(parents.shape, parents.dtype),
            pltpu.VMEM(ids.shape, ids.dtype),
            pltpu.VMEM(weights_of.shape, weights_of.dtype),
            pltpu.VMEM(queries.shape, queries.dtype),
            pltpu.VMEM(tree_kv.shape, tree_kv.dtype),
            pltpu.VMEM(kv_cache.shape, kv_cache.dtype),
            pltpu.VMEM(w_out.shape, w_out.dtype),
            pltpu.VMEM(w_gate.shape[1:], w_gate.dtype),
            pltpu.VMEM(w_up.shape[1:], w_up.dtype),
            pltpu.VMEM(w_down.shape[1:], w_down.dtype),
            pltpu.VMEM((slices, rows, queries.shape[1]), jnp.bfloat16),
            pltpu.VMEM((1 << starts[1], rows, features), jnp.float32),
            pltpu.VMEM((CHUNKS, count, rows, width), jnp.bfloat16),
            pltpu.VMEM((count, rows, lanes), jnp.float32),
            pltpu.VMEM((tiles, tile_rows, LANES), jnp.float32),
            pltpu.VMEM((tiles, tile_rows, hidden_width), jnp.float32),
            pltpu.VMEM((tiles, tile_rows, hidden_width), jnp.float32),
            pltpu.VMEM((tiles, tile_rows, hidden_width), jnp.bfloat16),
            pltpu.VMEM((count // 2, rows, features), jnp.float32),
            pltpu.VMEM((CHUNKS, slices, rows, width), jnp.bfloat16),
            pltpu.VMEM((CHUNKS, slices, rows, width), jnp.bfloat16),
            pltpu.VMEM((CHUNKS, count - 1, rows, width), jnp.bfloat16),
            pltpu.VMEM((CHUNKS, count - 1, rows, width), jnp.bfloat16),
            dma((12,)),
            dma((CHUNKS, near + 1)),
            dma((CHUNKS, near + 1)),
            dma((CHUNKS, links)),
            dma((CHUNKS, links)),
            dma((links,)),
            dma((links,)),
            dma((CHUNKS, links)),
            dma((CHUNKS, links)),
        ],
        compiler_params=pltpu.CompilerParams(
            collective_id=0, has_side_effects=True, vmem_limit_bytes=60 << 20
        ),
    )(
        block_table,
        cache_lengths,
        queries,
        tree_kv,
        kv_cache,
        parents,
        w_out,
        w_gate,
        w_up,
        w_down,
        ids,
        weights_of,
    )


def solution(mesh):
    placed = (
        P(("groups", "wide"), None),
        P(None, ("groups", "wide"), None),
        P(None, ("groups", "wide"), None, None),
        P(("groups", "wide"), None),
        P(("groups", "wide"), None),
        P(("groups", "wide"), None),
        P("wide", None),
        P("wide", None, None),
        P("wide", None, None),
        P("wide", None, None),
        P(("groups", "wide"), None),
        P(("groups", "wide"), None),
    )
    return jax.shard_map(
        body, mesh=mesh, in_specs=placed, out_specs=P(("groups", "wide"), None), check_vma=False
    )
```

time: 44.4 us -> 39.8 us (0.90)
  Pallas kernels: 42.7 us -> 39 us
  local copies, waits for them, and re-layouts: 1.47 us -> 0.63 us
    pallas_call x1, Pallas kernels: 42.7 us -> 39 us  [body(): pl.pallas_call(functools.partial(layer_kernel, count), out_shape=pltpu.VM...]
    unnamed x1, local copies, waits for them, and re-layouts: 1.47 us -> 0.63 us
where the time goes in v1:
time: 39.8 us; the launch traced here: 39.7 us
  Pallas kernels  39 us (98%)
  local copies, waits for them, and re-layouts  0.63 us (2%)
    pallas_call x1, Pallas kernels, body(): pl.pallas_call(functools.partial(layer_kernel, count), out_shape=pltpu.VM...  39 us

profile of v1, /device:TPU:0, one launch (start us, length us, event | category | flops | bytes accessed | tf_op | source)
XLA Modules:
  0.0 39.7 jit_solution(5732306594690314462)
XLA Ops:
  0.0 39.0 %shard_map.118 = bf16[16,2048]{1,0:T(8,128)(2,1)S(1)} custom-call(s32[4,4]{1,0:T(4,128)} %block_table_in.1, s32[1,4]{1,0:T(1,128)} %cache_lengths_in.1, bf16[128,512]{1,0:T(8,128)(2,1)} %queries_in.1, bf16[2,128,128]{2,1,0:T(8,128)(2,1)} %tree_in.1, bf16[2,16,32,128]{3,2,1,0:T(8,128)(2,1)} %cache_in.1, s32[4,32]{1,0:T(4,128)} %parents_in.1, ...), custom_call_target="tpu_custom_call" | custom-call | tf_op jit(solution)/shard_map/pallas_call | solution.py:536
  39.0 0.6 %copy.14 = bf16[16,2048]{1,0:T(8,128)(2,1)} copy(bf16[16,2048]{1,0:T(8,128)(2,1)S(1)} %shard_map.118) | data formatting | bytes 131072

commit v2 on v1

v2 whole, which is shorter than its diff:
```python
import functools

import jax
import jax.numpy as jnp
from jax import lax
from jax.experimental import pallas as pl
from jax.experimental.pallas import tpu as pltpu
from jax.sharding import PartitionSpec as P

CHUNKS = 4
DIRECT = 2
TILE = 256
LANES = 128
MESH = pl.DeviceIdType.MESH


def layout(count, slices):
    bits = list(range(count.bit_length() - 1))
    shift = len(bits) - (slices.bit_length() - 1)
    far, near = bits[-1:], bits[shift:-1]
    groups = [tuple(far), tuple(near)]
    low = bits[1:shift]
    while low:
        groups.append(tuple(low[-2:]))
        low = low[:-2]
    groups = [group for group in groups if group]
    starts = [0]
    for group in groups:
        starts.append(starts[-1] + len(group))
    return groups, starts, shift


def second_plans(starts):
    plan = list(zip(starts, starts[1:]))[::-1]
    short = [(0, starts[-1])] if len(starts) == 3 else plan
    return [short if chunk >= CHUNKS - DIRECT else plan for chunk in range(CHUNKS)]


def farthest_first(low, high):
    patterns = range(1, 1 << (high - low))
    return [p << low for p in sorted(patterns, key=lambda p: (-bin(p).count("1"), p))]


def layer_kernel(
    count,
    block_table_in,
    cache_lengths_in,
    queries_in,
    tree_in,
    cache_in,
    parents_in,
    w_out_in,
    w_gate_in,
    w_up_in,
    w_down_in,
    expert_ids_in,
    gate_weights_in,
    out,
    block_table,
    cache_lengths,
    parents,
    expert_ids,
    gate_weights,
    queries,
    tree,
    cache,
    w_out,
    w_gate,
    w_up,
    w_down,
    attended,
    partial,
    hidden,
    routing,
    row_weight,
    gate_sum,
    up_sum,
    activated,
    produced,
    send_one,
    recv_one,
    send_two,
    recv_two,
    load_sem,
    send_sem,
    one_recv_sem,
    all_recv_sem,
    route_recv_sem,
    two_recv_sem,
    twin_send_sem,
    twin_recv_sem,
):
    me = lax.axis_index("wide")
    rows = out.shape[0]
    slices = attended.shape[0]
    groups, starts, slice_shift = layout(count, slices)
    places = 1 << starts[-1]
    mine = [(me // (1 << bit)) % 2 for bit in range(starts[-1] + 1)]
    twin = me + 1 - 2 * mine[0]

    order = [bit for group in groups for bit in group]

    def peer(place):
        device = me
        for number, bit in enumerate(order):
            if place >> number & 1:
                device = device + (1 - 2 * mine[bit]) * (1 << bit)
        return device

    rounds = list(zip(starts, starts[1:]))
    plans = second_plans(starts)
    friends = sorted(
        {
            pattern << low
            for low, high in sum(plans, rounds)
            for pattern in range(1, 1 << (high - low))
        }
    )
    friends = [twin] + [peer(place) for place in friends]
    barrier = pltpu.get_barrier_semaphore()
    for friend in friends:
        pl.semaphore_signal(barrier, inc=1, device_id={"wide": friend}, device_id_type=MESH)

    loads = []
    for number, (source, target) in enumerate(
        (
            (parents_in, parents),
            (queries_in, queries),
            (tree_in, tree),
            (cache_in, cache),
            (block_table_in, block_table),
            (cache_lengths_in, cache_lengths),
            (expert_ids_in, expert_ids),
            (gate_weights_in, gate_weights),
            (w_out_in, w_out),
            (w_gate_in.at[0], w_gate.at[0]),
            (w_up_in.at[0], w_up.at[0]),
            (w_down_in.at[0], w_down.at[0]),
        )
    ):
        copy = pltpu.make_async_copy(source, target, load_sem.at[number])
        if number < 9:
            copy.start()
        loads.append(copy)

    seq_count, node_count = parents.shape
    head_dim = tree.shape[2]
    head_count = queries.shape[1] // head_dim
    page_count = block_table.shape[1]
    node_rows = lax.broadcasted_iota(jnp.int32, (node_count, node_count), 0)
    node_cols = lax.broadcasted_iota(jnp.int32, (node_count, node_count), 1)
    loads[0].wait()
    closures = []
    for seq in range(seq_count):
        linked = ((parents[seq : seq + 1, :] == node_rows) | (node_rows == node_cols)).astype(
            jnp.float32
        )
        closures.append(linked)
    for repeat in range(max(node_count - 1, 1).bit_length()):
        narrow = [linked.astype(jnp.bfloat16) for linked in closures]
        closures = [
            jnp.minimum(jnp.dot(linked, linked, preferred_element_type=jnp.float32), 1.0)
            for linked in narrow
        ]

    def relative_slice(place):
        index = 0
        for group, start in zip(groups, starts):
            for number, bit in enumerate(group):
                if bit >= slice_shift:
                    fixed = place >> (bit - slice_shift) & 1
                    index = index + (1 - mine[bit] if fixed else mine[bit]) * (
                        1 << (start + number)
                    )
        return index

    for copy in loads[1:6]:
        copy.wait()
    cached = page_count * cache.shape[2]
    positions = lax.broadcasted_iota(jnp.int32, (head_count * node_count, cached), 1)
    across = (((1,), (1,)), ((), ()))
    for seq in range(seq_count):
        first = seq * node_count
        last = first + node_count
        stacked = jnp.concatenate(
            [
                queries[first:last, head * head_dim : (head + 1) * head_dim]
                for head in range(head_count)
            ],
            axis=0,
        )
        pages = [block_table[seq, page] for page in range(page_count)]
        keys = jnp.concatenate([cache[0, page] for page in pages], axis=0)
        values = jnp.concatenate([cache[1, page] for page in pages], axis=0)
        scale = head_dim ** (-0.5)
        cache_scores = (
            lax.dot_general(stacked, keys, across, preferred_element_type=jnp.float32) * scale
        )
        tree_scores = (
            lax.dot_general(
                stacked, tree[0, first:last], across, preferred_element_type=jnp.float32
            )
            * scale
        )
        seen = jnp.concatenate([closures[seq].T] * head_count, axis=0) > 0.5
        cache_scores = jnp.where(positions < cache_lengths[0, seq], cache_scores, -jnp.inf)
        tree_scores = jnp.where(seen, tree_scores, -jnp.inf)
        highest = jnp.maximum(
            jnp.max(cache_scores, axis=1, keepdims=True),
            jnp.max(tree_scores, axis=1, keepdims=True),
        )
        cache_probs = jnp.exp(cache_scores - highest)
        tree_probs = jnp.exp(tree_scores - highest)
        denominator = jnp.sum(cache_probs, axis=1, keepdims=True) + jnp.sum(
            tree_probs, axis=1, keepdims=True
        )
        blended = jnp.dot(
            cache_probs.astype(jnp.bfloat16), values, preferred_element_type=jnp.float32
        ) + jnp.dot(
            tree_probs.astype(jnp.bfloat16),
            tree[1, first:last],
            preferred_element_type=jnp.float32,
        )
        blended = (blended / denominator).astype(jnp.bfloat16)
        for part in range(node_count // rows):
            index = relative_slice((first + part * rows) // rows)
            for head in range(head_count):
                top = head * node_count + part * rows
                attended[index, :, head * head_dim : (head + 1) * head_dim] = blended[
                    top : top + rows
                ]

    def send(source, target, send_sem, recv_sem, device):
        pltpu.make_async_remote_copy(
            src_ref=source,
            dst_ref=target,
            send_sem=send_sem,
            recv_sem=recv_sem,
            device_id={"wide": device},
            device_id_type=MESH,
        ).start()

    def await_bytes(view, sem):
        pltpu.make_async_copy(view, view, sem).wait()

    width = w_out.shape[1] // CHUNKS
    spans = [slice(chunk * width, (chunk + 1) * width) for chunk in range(CHUNKS)]

    class Gather:
        def __init__(self, buffer, send_sem, recv_sems):
            self.buffer = buffer
            self.send_sem = send_sem
            self.recv_sems = recv_sems

        def start(self, step):
            held = 1 << starts[step]
            for place in farthest_first(*rounds[step]):
                send(
                    self.buffer.at[pl.ds(0, held)],
                    self.buffer.at[pl.ds(place, held)],
                    self.send_sem,
                    self.recv_sems.at[step],
                    peer(place),
                )

        def finish(self, step):
            held = 1 << starts[step]
            region = pl.ds(held, (1 << starts[step + 1]) - held)
            await_bytes(self.buffer.at[region], self.recv_sems.at[step])

    class Scatter:
        def __init__(self, kept, out_buffer, in_buffer, send_sem, recv_sems, plans):
            self.kept = kept
            self.out_buffer = out_buffer
            self.in_buffer = in_buffer
            self.send_sem = send_sem
            self.recv_sems = recv_sems
            self.plans = plans

        def slot(self, chunk, turn, place):
            plan = self.plans[chunk]
            first = sum((1 << high) - (1 << low) for low, high in plan[:turn])
            return first + place - (1 << plan[turn][0])

        def launch(self, chunk, turn, place):
            held = 1 << self.plans[chunk][turn][0]
            region = pl.ds(self.slot(chunk, turn, place), held)
            send(
                self.out_buffer.at[chunk, region],
                self.in_buffer.at[chunk, region],
                self.send_sem,
                self.recv_sems.at[chunk, turn],
                peer(place),
            )

        def start(self, chunk, turn, value):
            low, high = self.plans[chunk][turn]
            for first in farthest_first(low, high):
                for place in range(first, first + (1 << low)):
                    self.out_buffer[chunk, self.slot(chunk, turn, place)] = value(place).astype(
                        jnp.bfloat16
                    )
                self.launch(chunk, turn, first)
            for place in range(1 << low):
                self.kept[place, :, spans[chunk]] = value(place)

        def finish(self, chunk, turn):
            low, high = self.plans[chunk][turn]
            region = pl.ds(self.slot(chunk, turn, 1 << low), (1 << high) - (1 << low))
            await_bytes(self.in_buffer.at[chunk, region], self.recv_sems.at[chunk, turn])

        def value(self, chunk, turn, place):
            low, high = self.plans[chunk][turn]
            total = self.kept[place, :, spans[chunk]]
            for first in range(1 << low, 1 << high, 1 << low):
                total = total + self.in_buffer[
                    chunk, self.slot(chunk, turn, first + place)
                ].astype(jnp.float32)
            return total

    far_step, near_step, last_step = 0, 1, len(groups) - 1
    first_sum = Scatter(partial, send_one, recv_one, send_sem.at[0], one_recv_sem,
        [[rounds[near_step]]] * CHUNKS)
    second_sum = Scatter(
        produced, send_two, recv_two, send_sem.at[1], two_recv_sem,
        plans,
    )
    gathers = [
        Gather(hidden.at[chunk], send_sem.at[2], all_recv_sem.at[chunk])
        for chunk in range(CHUNKS)
    ]
    route = Gather(routing, send_sem.at[3], route_recv_sem)

    loads[8].wait()
    for copy in loads[9:]:
        copy.start()
    for chunk in range(CHUNKS):
        projected = jnp.dot(
            attended[...].reshape(slices * rows, attended.shape[2]),
            w_out[:, spans[chunk]],
            preferred_element_type=jnp.float32,
        )
        if chunk == 0:
            pl.semaphore_wait(barrier, len(friends))
        first_sum.start(
            chunk, 0, lambda place: projected[place * rows : (place + 1) * rows]
        )
    loads[6].wait()
    loads[7].wait()
    ids = expert_ids[...].T
    weights_of = gate_weights[...].T
    lane_ids = lax.broadcasted_iota(jnp.int32, (rows, routing.shape[2]), 1)
    listed = jnp.zeros((rows, routing.shape[2]), jnp.float32)
    for k in range(expert_ids.shape[0]):
        listed += jnp.where(ids[:, k : k + 1] == lane_ids, weights_of[:, k : k + 1], 0.0)
    routing[0] = listed

    route.start(far_step)
    for number, (source, target) in enumerate(
        ((w_gate_in, w_gate), (w_up_in, w_up), (w_down_in, w_down))
    ):
        send(source.at[0], target.at[1], twin_send_sem.at[number], twin_recv_sem.at[number], twin)

    held = 1 << starts[near_step]
    far_base = (slices - held)
    for chunk in range(CHUNKS):
        first_sum.finish(chunk, 0)
        for place in range(held):
            value = first_sum.value(chunk, 0, place)
            partial[place, :, spans[chunk]] = value
            send_one[chunk, far_base + held - 1 - place] = value.astype(jnp.bfloat16)
        region = pl.ds(far_base, held)
        send(
            send_one.at[chunk, region],
            recv_one.at[chunk, region],
            send_sem.at[0],
            one_recv_sem.at[chunk, 1],
            peer(1),
        )
    route.finish(far_step)
    route.start(near_step)
    for chunk in range(CHUNKS):
        await_bytes(
            recv_one.at[chunk, pl.ds(far_base, held)], one_recv_sem.at[chunk, 1]
        )
        for place in range(held):
            hidden[chunk, place] = (
                partial[place, :, spans[chunk]]
                + recv_one[chunk, far_base + place].astype(jnp.float32)
            ).astype(jnp.bfloat16)
        gathers[chunk].start(near_step)

    for step in range(near_step, last_step):
        route.finish(step)
        route.start(step + 1)
        if step + 1 < last_step:
            for chunk in range(CHUNKS):
                gathers[chunk].finish(step)
                gathers[chunk].start(step + 1)

    hidden_width = w_gate.shape[2]
    tiles, tile_rows = activated.shape[1:3]
    tile_blocks = tile_rows // rows
    cuts = [
        slice(start, min(start + TILE, hidden_width)) for start in range(0, hidden_width, TILE)
    ]

    def over_tiles(step):
        if tiles == 1:
            step(0)
        else:
            pl.loop(0, tiles)(step)

    def weigh(tile):
        table = routing[pl.ds(tile * tile_blocks, tile_blocks)].reshape(
            tile_rows, routing.shape[2]
        )
        experts = lax.broadcasted_iota(jnp.int32, table.shape, 1)
        for number, expert in enumerate((me, twin)):
            weight = jnp.sum(jnp.where(experts == expert, table, 0.0), axis=1, keepdims=True)
            row_weight[number, tile] = jnp.broadcast_to(weight, (tile_rows, LANES))

    for chunk in range(CHUNKS):
        gathers[chunk].finish(last_step)
        if chunk == 0:
            for number, weights in enumerate((w_gate, w_up)):
                loads[9 + number].wait()
                await_bytes(weights.at[1], twin_recv_sem.at[number])

        def accumulate(tile, chunk=chunk):
            taken = hidden[chunk, pl.ds(tile * tile_blocks, tile_blocks)].reshape(
                tile_rows, width
            )
            for number in range(2):
                for cut in cuts:
                    for sums, weights in ((gate_sum, w_gate), (up_sum, w_up)):
                        part = jnp.dot(
                            taken,
                            weights[number, spans[chunk], cut],
                            preferred_element_type=jnp.float32,
                        )
                        if chunk == 0:
                            sums[number, tile, :, cut] = part
                        else:
                            sums[number, tile, :, cut] += part

        over_tiles(accumulate)
        if chunk == 0:
            route.finish(last_step)
            over_tiles(weigh)

    def activate(tile):
        for number in range(2):
            for cut in cuts:
                gate = gate_sum[number, tile, :, cut]
                activated[number, tile, :, cut] = (
                    gate / (1.0 + jnp.exp(-gate)) * up_sum[number, tile, :, cut]
                ).astype(jnp.bfloat16)

    over_tiles(activate)
    loads[11].wait()
    await_bytes(w_down.at[1], twin_recv_sem.at[2])

    def down(chunk, tile):
        total = None
        for number in range(2):
            made = jnp.dot(
                activated[number, tile],
                w_down[number, :, spans[chunk]],
                preferred_element_type=jnp.float32,
            )
            weighed = made * jnp.concatenate(
                [row_weight[number, tile]] * (width // LANES), axis=1
            )
            total = weighed if total is None else total + weighed
        return total.reshape(tile_blocks, rows, width)

    for chunk in range(CHUNKS):
        made = [down(chunk, tile) for tile in range(tiles)]
        second_sum.start(
            chunk, 0, lambda place: made[place // tile_blocks][place % tile_blocks]
        )
    for turn in range(len(rounds)):
        for chunk in range(CHUNKS):
            turns = len(plans[chunk])
            if turn >= turns:
                continue
            second_sum.finish(chunk, turn)
            if turn + 1 < turns:
                second_sum.start(
                    chunk, turn + 1, functools.partial(second_sum.value, chunk, turn)
                )
            else:
                out[:, spans[chunk]] = second_sum.value(chunk, turn, 0).astype(jnp.bfloat16)
    await_bytes(send_one, send_sem.at[0])
    await_bytes(send_two, send_sem.at[1])
    given = sum(
        ((1 << len(groups[step])) - 1) << starts[step] for step in range(near_step, last_step + 1)
    )
    await_bytes(hidden.at[:, pl.ds(0, given)], send_sem.at[2])
    await_bytes(routing.at[pl.ds(1, places - 1)], send_sem.at[3])
    for number, weights in enumerate((w_gate, w_up, w_down)):
        await_bytes(weights.at[0], twin_send_sem.at[number])


def body(
    queries,
    tree_kv,
    kv_cache,
    block_table,
    cache_lengths,
    parents,
    w_out,
    w_gate,
    w_up,
    w_down,
    expert_ids,
    gate_weights,
):
    count = lax.axis_size("wide")
    rows = expert_ids.shape[0]
    features = w_out.shape[1]
    hidden_width = w_gate.shape[2]
    slices = queries.shape[0] // rows
    groups, starts, slice_shift = layout(count, slices)
    width = features // CHUNKS
    lanes = -(-count // LANES) * LANES
    places = 1 << starts[-1]
    tile_rows = min(TILE, places * rows)
    tiles = places * rows // tile_rows
    hbm = pl.BlockSpec(memory_space=pl.ANY)
    vmem = pl.BlockSpec(memory_space=pltpu.VMEM)
    dma = pltpu.SemaphoreType.DMA
    ids, weights_of = expert_ids.T, gate_weights.T
    return pl.pallas_call(
        functools.partial(layer_kernel, count),
        out_shape=pltpu.VMEM((rows, features), jnp.bfloat16),
        in_specs=[hbm] * 12,
        out_specs=vmem,
        scratch_shapes=[
            pltpu.SMEM(block_table.shape, block_table.dtype),
            pltpu.SMEM(cache_lengths.shape, cache_lengths.dtype),
            pltpu.VMEM(parents.shape, parents.dtype),
            pltpu.VMEM(ids.shape, ids.dtype),
            pltpu.VMEM(weights_of.shape, weights_of.dtype),
            pltpu.VMEM(queries.shape, queries.dtype),
            pltpu.VMEM(tree_kv.shape, tree_kv.dtype),
            pltpu.VMEM(kv_cache.shape, kv_cache.dtype),
            pltpu.VMEM(w_out.shape, w_out.dtype),
            pltpu.VMEM((2, *w_gate.shape[1:]), w_gate.dtype),
            pltpu.VMEM((2, *w_up.shape[1:]), w_up.dtype),
            pltpu.VMEM((2, *w_down.shape[1:]), w_down.dtype),
            pltpu.VMEM((slices, rows, queries.shape[1]), jnp.bfloat16),
            pltpu.VMEM((1 << starts[1], rows, features), jnp.float32),
            pltpu.VMEM((CHUNKS, places, rows, width), jnp.bfloat16),
            pltpu.VMEM((places, rows, lanes), jnp.float32),
            pltpu.VMEM((2, tiles, tile_rows, LANES), jnp.float32),
            pltpu.VMEM((2, tiles, tile_rows, hidden_width), jnp.float32),
            pltpu.VMEM((2, tiles, tile_rows, hidden_width), jnp.float32),
            pltpu.VMEM((2, tiles, tile_rows, hidden_width), jnp.bfloat16),
            pltpu.VMEM((1 << starts[-2], rows, features), jnp.float32),
            pltpu.VMEM((CHUNKS, slices, rows, width), jnp.bfloat16),
            pltpu.VMEM((CHUNKS, slices, rows, width), jnp.bfloat16),
            pltpu.VMEM((CHUNKS, places - 1, rows, width), jnp.bfloat16),
            pltpu.VMEM((CHUNKS, places - 1, rows, width), jnp.bfloat16),
            dma((12,)),
            dma((4,)),
            dma((CHUNKS, 2)),
            dma((CHUNKS, len(groups))),
            dma((len(groups),)),
            dma((CHUNKS, len(groups))),
            dma((3,)),
            dma((3,)),
        ],
        compiler_params=pltpu.CompilerParams(
            collective_id=0, has_side_effects=True, vmem_limit_bytes=60 << 20
        ),
    )(
        block_table,
        cache_lengths,
        queries,
        tree_kv,
        kv_cache,
        parents,
        w_out,
        w_gate,
        w_up,
        w_down,
        ids,
        weights_of,
    )


def solution(mesh):
    placed = (
        P(("groups", "wide"), None),
        P(None, ("groups", "wide"), None),
        P(None, ("groups", "wide"), None, None),
        P(("groups", "wide"), None),
        P(("groups", "wide"), None),
        P(("groups", "wide"), None),
        P("wide", None),
        P("wide", None, None),
        P("wide", None, None),
        P("wide", None, None),
        P(("groups", "wide"), None),
        P(("groups", "wide"), None),
    )
    return jax.shard_map(
        body, mesh=mesh, in_specs=placed, out_specs=P(("groups", "wide"), None), check_vma=False
    )
```

time: 39.8 us -> 33.7 us (0.85)
  Pallas kernels: 39 us -> 32.9 us
    pallas_call x1, Pallas kernels: 39 us -> 32.9 us  [body(): pl.pallas_call(functools.partial(layer_kernel, count), out_shape=pltpu.VM...]
where the time goes in v2:
time: 33.7 us; the launch traced here: 33.5 us
  Pallas kernels  32.9 us (98%)
  local copies, waits for them, and re-layouts  0.63 us (2%)
    pallas_call x1, Pallas kernels, body(): pl.pallas_call(functools.partial(layer_kernel, count), out_shape=pltpu.VM...  32.9 us

profile of v2, /device:TPU:0, one launch (start us, length us, event | category | flops | bytes accessed | tf_op | source)
XLA Modules:
  0.0 33.5 jit_solution(12474420843631814517)
XLA Ops:
  0.0 32.9 %shard_map.118 = bf16[16,2048]{1,0:T(8,128)(2,1)S(1)} custom-call(s32[4,4]{1,0:T(4,128)} %block_table_in.1, s32[1,4]{1,0:T(1,128)} %cache_lengths_in.1, bf16[128,512]{1,0:T(8,128)(2,1)} %queries_in.1, bf16[2,128,128]{2,1,0:T(8,128)(2,1)} %tree_in.1, bf16[2,16,32,128]{3,2,1,0:T(8,128)(2,1)} %cache_in.1, s32[4,32]{1,0:T(4,128)} %parents_in.1, ...), custom_call_target="tpu_custom_call" | custom-call | tf_op jit(solution)/shard_map/pallas_call | solution.py:535
  32.9 0.6 %copy.14 = bf16[16,2048]{1,0:T(8,128)(2,1)} copy(bf16[16,2048]{1,0:T(8,128)(2,1)S(1)} %shard_map.118) | data formatting | bytes 131072

commit v3 on v2

--- a/solution.py
+++ b/solution.py
@@ -7,8 +7,10 @@
 from jax.experimental.pallas import tpu as pltpu
 from jax.sharding import PartitionSpec as P
 
-CHUNKS = 4
+FRONT = (3, 5, 5, 3)
+BACK = (4, 4, 4, 4)
 DIRECT = 2
+CHUNKS = len(FRONT)
 TILE = 256
 LANES = 128
 MESH = pl.DeviceIdType.MESH
@@ -33,12 +35,27 @@
 def second_plans(starts):
     plan = list(zip(starts, starts[1:]))[::-1]
     short = [(0, starts[-1])] if len(starts) == 3 else plan
-    return [short if chunk >= CHUNKS - DIRECT else plan for chunk in range(CHUNKS)]
+    return [short if chunk >= len(BACK) - DIRECT else plan for chunk in range(len(BACK))]
+
+
+def shares_of(features, shares):
+    spans, start = [], 0
+    for share in shares:
+        stop = start + share * features // sum(shares)
+        spans.append(slice(start, stop))
+        start = stop
+    return spans
+
+
+def widest_of(features, shares):
+    return max(span.stop - span.start for span in shares_of(features, shares))
 
 
 def farthest_first(low, high):
-    patterns = range(1, 1 << (high - low))
-    return [p << low for p in sorted(patterns, key=lambda p: (-bin(p).count("1"), p))]
+    def distance(place):
+        return (-(place & 1), -bin(place).count("1"), place)
+
+    return sorted(range(1 << low, 1 << high, 1 << low), key=distance)
 
 
 def layer_kernel(
@@ -132,16 +149,21 @@
             (cache_lengths_in, cache_lengths),
             (expert_ids_in, expert_ids),
             (gate_weights_in, gate_weights),
-            (w_out_in, w_out),
             (w_gate_in.at[0], w_gate.at[0]),
             (w_up_in.at[0], w_up.at[0]),
             (w_down_in.at[0], w_down.at[0]),
         )
     ):
         copy = pltpu.make_async_copy(source, target, load_sem.at[number])
-        if number < 9:
+        if number < 6:
             copy.start()
         loads.append(copy)
+    out_loads = []
+    for number, span in enumerate(shares_of(w_out.shape[1], FRONT)):
+        view = (slice(None), pl.ds(span.start, span.stop - span.start))
+        out_loads.append(
+            pltpu.make_async_copy(w_out_in.at[view], w_out.at[view], load_sem.at[11 + number])
+        )
 
     seq_count, node_count = parents.shape
     head_dim = tree.shape[2]
@@ -150,6 +172,8 @@
     node_rows = lax.broadcasted_iota(jnp.int32, (node_count, node_count), 0)
     node_cols = lax.broadcasted_iota(jnp.int32, (node_count, node_count), 1)
     loads[0].wait()
+    for copy in out_loads + loads[6:8]:
+        copy.start()
     closures = []
     for seq in range(seq_count):
         linked = ((parents[seq : seq + 1, :] == node_rows) | (node_rows == node_cols)).astype(
@@ -159,8 +183,7 @@
     for repeat in range(max(node_count - 1, 1).bit_length()):
         narrow = [linked.astype(jnp.bfloat16) for linked in closures]
         closures = [
-            jnp.minimum(jnp.dot(linked, linked, preferred_element_type=jnp.float32), 1.0)
-            for linked in narrow
+            jnp.dot(linked, linked, preferred_element_type=jnp.float32) for linked in narrow
         ]
 
     def relative_slice(place):
@@ -173,6 +196,25 @@
                         1 << (start + number)
                     )
         return index
+
+    def send(source, target, send_sem, recv_sem, device):
+        pltpu.make_async_remote_copy(
+            src_ref=source,
+            dst_ref=target,
+            send_sem=send_sem,
+            recv_sem=recv_sem,
+            device_id={"wide": device},
+            device_id_type=MESH,
+        ).start()
+
+    def await_bytes(view, sem):
+        pltpu.make_async_copy(view, view, sem).wait()
+
+    shared = ((w_gate_in, w_gate), (w_up_in, w_up), (w_down_in, w_down))
+
+    def share(number):
+        source, target = shared[number]
+        send(source.at[0], target.at[1], twin_send_sem.at[number], twin_recv_sem.at[number], twin)
 
     for copy in loads[1:6]:
         copy.wait()
@@ -230,21 +272,9 @@
                     top : top + rows
                 ]
 
-    def send(source, target, send_sem, recv_sem, device):
-        pltpu.make_async_remote_copy(
-            src_ref=source,
-            dst_ref=target,
-            send_sem=send_sem,
-            recv_sem=recv_sem,
-            device_id={"wide": device},
-            device_id_type=MESH,
-        ).start()
-
-    def await_bytes(view, sem):
-        pltpu.make_async_copy(view, view, sem).wait()
-
-    width = w_out.shape[1] // CHUNKS
-    spans = [slice(chunk * width, (chunk + 1) * width) for chunk in range(CHUNKS)]
+    spans = shares_of(w_out.shape[1], FRONT)
+    columns = [pl.ds(0, span.stop - span.start) for span in spans]
+    back_spans = shares_of(w_out.shape[1], BACK)
 
     class Gather:
         def __init__(self, buffer, send_sem, recv_sems):
@@ -269,13 +299,15 @@
             await_bytes(self.buffer.at[region], self.recv_sems.at[step])
 
     class Scatter:
-        def __init__(self, kept, out_buffer, in_buffer, send_sem, recv_sems, plans):
+        def __init__(self, kept, out_buffer, in_buffer, send_sem, recv_sems, plans, spans):
+            self.spans = spans
             self.kept = kept
             self.out_buffer = out_buffer
             self.in_buffer = in_buffer
             self.send_sem = send_sem
             self.recv_sems = recv_sems
             self.plans = plans
+            self.columns = [pl.ds(0, span.stop - span.start) for span in spans]
 
         def slot(self, chunk, turn, place):
             plan = self.plans[chunk]
@@ -286,8 +318,8 @@
             held = 1 << self.plans[chunk][turn][0]
             region = pl.ds(self.slot(chunk, turn, place), held)
             send(
-                self.out_buffer.at[chunk, region],
-                self.in_buffer.at[chunk, region],
+                self.out_buffer.at[chunk, region, :, self.columns[chunk]],
+                self.in_buffer.at[chunk, region, :, self.columns[chunk]],
                 self.send_sem,
                 self.recv_sems.at[chunk, turn],
                 peer(place),
@@ -297,51 +329,54 @@
             low, high = self.plans[chunk][turn]
             for first in farthest_first(low, high):
                 for place in range(first, first + (1 << low)):
-                    self.out_buffer[chunk, self.slot(chunk, turn, place)] = value(place).astype(
-                        jnp.bfloat16
-                    )
+                    self.out_buffer[
+                        chunk, self.slot(chunk, turn, place), :, self.columns[chunk]
+                    ] = value(place).astype(jnp.bfloat16)
                 self.launch(chunk, turn, first)
             for place in range(1 << low):
-                self.kept[place, :, spans[chunk]] = value(place)
+                self.kept[place, :, self.spans[chunk]] = value(place)
 
         def finish(self, chunk, turn):
             low, high = self.plans[chunk][turn]
             region = pl.ds(self.slot(chunk, turn, 1 << low), (1 << high) - (1 << low))
-            await_bytes(self.in_buffer.at[chunk, region], self.recv_sems.at[chunk, turn])
+            await_bytes(
+                self.in_buffer.at[chunk, region, :, self.columns[chunk]],
+                self.recv_sems.at[chunk, turn],
+            )
 
         def value(self, chunk, turn, place):
             low, high = self.plans[chunk][turn]
-            total = self.kept[place, :, spans[chunk]]
+            total = self.kept[place, :, self.spans[chunk]]
             for first in range(1 << low, 1 << high, 1 << low):
                 total = total + self.in_buffer[
-                    chunk, self.slot(chunk, turn, first + place)
+                    chunk, self.slot(chunk, turn, first + place), :, self.columns[chunk]
                 ].astype(jnp.float32)
             return total
 
     far_step, near_step, last_step = 0, 1, len(groups) - 1
     first_sum = Scatter(partial, send_one, recv_one, send_sem.at[0], one_recv_sem,
-        [[rounds[near_step]]] * CHUNKS)
+        [[rounds[near_step]]] * CHUNKS, spans,
+    )
     second_sum = Scatter(
         produced, send_two, recv_two, send_sem.at[1], two_recv_sem,
-        plans,
+        plans, back_spans,
     )
     gathers = [
-        Gather(hidden.at[chunk], send_sem.at[2], all_recv_sem.at[chunk])
+        Gather(hidden.at[chunk, :, :, columns[chunk]], send_sem.at[2], all_recv_sem.at[chunk])
         for chunk in range(CHUNKS)
     ]
     route = Gather(routing, send_sem.at[3], route_recv_sem)
 
-    loads[8].wait()
-    for copy in loads[9:]:
-        copy.start()
+    pl.semaphore_wait(barrier, len(friends))
+    share(0)
+    share(1)
     for chunk in range(CHUNKS):
+        out_loads[chunk].wait()
         projected = jnp.dot(
             attended[...].reshape(slices * rows, attended.shape[2]),
             w_out[:, spans[chunk]],
             preferred_element_type=jnp.float32,
         )
-        if chunk == 0:
-            pl.semaphore_wait(barrier, len(friends))
         first_sum.start(
             chunk, 0, lambda place: projected[place * rows : (place + 1) * rows]
         )
@@ -356,10 +391,8 @@
     routing[0] = listed
 
     route.start(far_step)
-    for number, (source, target) in enumerate(
-        ((w_gate_in, w_gate), (w_up_in, w_up), (w_down_in, w_down))
-    ):
-        send(source.at[0], target.at[1], twin_send_sem.at[number], twin_recv_sem.at[number], twin)
+    for copy in loads[8:]:
+        copy.start()
 
     held = 1 << starts[near_step]
     far_base = (slices - held)
@@ -368,25 +401,29 @@
         for place in range(held):
             value = first_sum.value(chunk, 0, place)
             partial[place, :, spans[chunk]] = value
-            send_one[chunk, far_base + held - 1 - place] = value.astype(jnp.bfloat16)
+            send_one[chunk, far_base + held - 1 - place, :, columns[chunk]] = value.astype(
+                jnp.bfloat16
+            )
         region = pl.ds(far_base, held)
         send(
-            send_one.at[chunk, region],
-            recv_one.at[chunk, region],
+            send_one.at[chunk, region, :, columns[chunk]],
+            recv_one.at[chunk, region, :, columns[chunk]],
             send_sem.at[0],
             one_recv_sem.at[chunk, 1],
             peer(1),
         )
+    share(2)
     route.finish(far_step)
     route.start(near_step)
     for chunk in range(CHUNKS):
         await_bytes(
-            recv_one.at[chunk, pl.ds(far_base, held)], one_recv_sem.at[chunk, 1]
+            recv_one.at[chunk, pl.ds(far_base, held), :, columns[chunk]],
+            one_recv_sem.at[chunk, 1],
         )
         for place in range(held):
-            hidden[chunk, place] = (
+            hidden[chunk, place, :, columns[chunk]] = (
                 partial[place, :, spans[chunk]]
-                + recv_one[chunk, far_base + place].astype(jnp.float32)
+                + recv_one[chunk, far_base + place, :, columns[chunk]].astype(jnp.float32)
             ).astype(jnp.bfloat16)
         gathers[chunk].start(near_step)
 
@@ -424,19 +461,19 @@
         gathers[chunk].finish(last_step)
         if chunk == 0:
             for number, weights in enumerate((w_gate, w_up)):
-                loads[9 + number].wait()
+                loads[8 + number].wait()
                 await_bytes(weights.at[1], twin_recv_sem.at[number])
 
         def accumulate(tile, chunk=chunk):
-            taken = hidden[chunk, pl.ds(tile * tile_blocks, tile_blocks)].reshape(
-                tile_rows, width
-            )
+            span = spans[chunk]
+            taken = hidden[chunk, pl.ds(tile * tile_blocks, tile_blocks), :, columns[chunk]]
+            taken = taken.reshape(tile_rows, span.stop - span.start)
             for number in range(2):
                 for cut in cuts:
                     for sums, weights in ((gate_sum, w_gate), (up_sum, w_up)):
                         part = jnp.dot(
                             taken,
-                            weights[number, spans[chunk], cut],
+                            weights[number, span, cut],
                             preferred_element_type=jnp.float32,
                         )
                         if chunk == 0:
@@ -458,7 +495,7 @@
                 ).astype(jnp.bfloat16)
 
     over_tiles(activate)
-    loads[11].wait()
+    loads[10].wait()
     await_bytes(w_down.at[1], twin_recv_sem.at[2])
 
     def down(chunk, tile):
@@ -466,22 +503,22 @@
         for number in range(2):
             made = jnp.dot(
                 activated[number, tile],
-                w_down[number, :, spans[chunk]],
+                w_down[number, :, back_spans[chunk]],
                 preferred_element_type=jnp.float32,
             )
             weighed = made * jnp.concatenate(
-                [row_weight[number, tile]] * (width // LANES), axis=1
+                [row_weight[number, tile]] * (made.shape[1] // LANES), axis=1
             )
             total = weighed if total is None else total + weighed
-        return total.reshape(tile_blocks, rows, width)
-
-    for chunk in range(CHUNKS):
+        return total.reshape(tile_blocks, rows, total.shape[1])
+
+    for chunk in range(len(BACK)):
         made = [down(chunk, tile) for tile in range(tiles)]
         second_sum.start(
             chunk, 0, lambda place: made[place // tile_blocks][place % tile_blocks]
         )
     for turn in range(len(rounds)):
-        for chunk in range(CHUNKS):
+        for chunk in range(len(BACK)):
             turns = len(plans[chunk])
             if turn >= turns:
                 continue
@@ -491,13 +528,16 @@
                     chunk, turn + 1, functools.partial(second_sum.value, chunk, turn)
                 )
             else:
-                out[:, spans[chunk]] = second_sum.value(chunk, turn, 0).astype(jnp.bfloat16)
-    await_bytes(send_one, send_sem.at[0])
-    await_bytes(send_two, send_sem.at[1])
+                out[:, back_spans[chunk]] = second_sum.value(chunk, turn, 0).astype(jnp.bfloat16)
+    for chunk in range(CHUNKS):
+        await_bytes(send_one.at[chunk, :, :, columns[chunk]], send_sem.at[0])
+    for chunk, span in enumerate(back_spans):
+        await_bytes(send_two.at[chunk, :, :, pl.ds(0, span.stop - span.start)], send_sem.at[1])
     given = sum(
         ((1 << len(groups[step])) - 1) << starts[step] for step in range(near_step, last_step + 1)
     )
-    await_bytes(hidden.at[:, pl.ds(0, given)], send_sem.at[2])
+    for chunk in range(CHUNKS):
+        await_bytes(hidden.at[chunk, pl.ds(0, given), :, columns[chunk]], send_sem.at[2])
     await_bytes(routing.at[pl.ds(1, places - 1)], send_sem.at[3])
     for number, weights in enumerate((w_gate, w_up, w_down)):
         await_bytes(weights.at[0], twin_send_sem.at[number])
@@ -523,7 +563,7 @@
     hidden_width = w_gate.shape[2]
     slices = queries.shape[0] // rows
     groups, starts, slice_shift = layout(count, slices)
-    width = features // CHUNKS
+    front, back = widest_of(features, FRONT), widest_of(features, BACK)
     lanes = -(-count // LANES) * LANES
     places = 1 << starts[-1]
     tile_rows = min(TILE, places * rows)
@@ -552,23 +592,23 @@
             pltpu.VMEM((2, *w_down.shape[1:]), w_down.dtype),
             pltpu.VMEM((slices, rows, queries.shape[1]), jnp.bfloat16),
             pltpu.VMEM((1 << starts[1], rows, features), jnp.float32),
-            pltpu.VMEM((CHUNKS, places, rows, width), jnp.bfloat16),
+            pltpu.VMEM((CHUNKS, places, rows, front), jnp.bfloat16),
             pltpu.VMEM((places, rows, lanes), jnp.float32),
             pltpu.VMEM((2, tiles, tile_rows, LANES), jnp.float32),
             pltpu.VMEM((2, tiles, tile_rows, hidden_width), jnp.float32),
             pltpu.VMEM((2, tiles, tile_rows, hidden_width), jnp.float32),
             pltpu.VMEM((2, tiles, tile_rows, hidden_width), jnp.bfloat16),
             pltpu.VMEM((1 << starts[-2], rows, features), jnp.float32),
-            pltpu.VMEM((CHUNKS, slices, rows, width), jnp.bfloat16),
-            pltpu.VMEM((CHUNKS, slices, rows, width), jnp.bfloat16),
-            pltpu.VMEM((CHUNKS, places - 1, rows, width), jnp.bfloat16),
-            pltpu.VMEM((CHUNKS, places - 1, rows, width), jnp.bfloat16),
-            dma((12,)),
+            pltpu.VMEM((CHUNKS, slices, rows, front), jnp.bfloat16),
+            pltpu.VMEM((CHUNKS, slices, rows, front), jnp.bfloat16),
+            pltpu.VMEM((len(BACK), places - 1, rows, back), jnp.bfloat16),
+            pltpu.VMEM((len(BACK), places - 1, rows, back), jnp.bfloat16),
+            dma((11 + CHUNKS,)),
             dma((4,)),
             dma((CHUNKS, 2)),
             dma((CHUNKS, len(groups))),
             dma((len(groups),)),
-            dma((CHUNKS, len(groups))),
+            dma((len(BACK), len(groups))),
             dma((3,)),
             dma((3,)),
         ],

time: 33.7 us -> 33.5 us (level)
  no operation moved by 1% of the time
where the time goes in v3:
time: 33.5 us; the launch traced here: 33.3 us
  Pallas kernels  32.7 us (98%)
  local copies, waits for them, and re-layouts  0.63 us (2%)
    pallas_call x1, Pallas kernels, body(): pl.pallas_call(functools.partial(layer_kernel, count), out_shape=pltpu.VM...  32.7 us

profile of v3, /device:TPU:0, one launch (start us, length us, event | category | flops | bytes accessed | tf_op | source)
XLA Modules:
  0.0 33.3 jit_solution(2614301464119667473)
XLA Ops:
  0.0 32.7 %shard_map.118 = bf16[16,2048]{1,0:T(8,128)(2,1)S(1)} custom-call(s32[4,4]{1,0:T(4,128)} %block_table_in.1, s32[1,4]{1,0:T(1,128)} %cache_lengths_in.1, bf16[128,512]{1,0:T(8,128)(2,1)} %queries_in.1, bf16[2,128,128]{2,1,0:T(8,128)(2,1)} %tree_in.1, bf16[2,16,32,128]{3,2,1,0:T(8,128)(2,1)} %cache_in.1, s32[4,32]{1,0:T(4,128)} %parents_in.1, ...), custom_call_target="tpu_custom_call" | custom-call | tf_op jit(solution)/shard_map/pallas_call | solution.py:575
  32.7 0.6 %copy.14 = bf16[16,2048]{1,0:T(8,128)(2,1)} copy(bf16[16,2048]{1,0:T(8,128)(2,1)S(1)} %shard_map.118) | data formatting | bytes 131072

commit v4 on v3

--- a/solution.py
+++ b/solution.py
@@ -277,7 +277,8 @@
     back_spans = shares_of(w_out.shape[1], BACK)
 
     class Gather:
-        def __init__(self, buffer, send_sem, recv_sems):
+        def __init__(self, buffer, send_sem, recv_sems, skipped):
+            self.skipped = skipped
             self.buffer = buffer
             self.send_sem = send_sem
             self.recv_sems = recv_sems
@@ -289,14 +290,14 @@
                     self.buffer.at[pl.ds(0, held)],
                     self.buffer.at[pl.ds(place, held)],
                     self.send_sem,
-                    self.recv_sems.at[step],
+                    self.recv_sems.at[step - self.skipped],
                     peer(place),
                 )
 
         def finish(self, step):
             held = 1 << starts[step]
             region = pl.ds(held, (1 << starts[step + 1]) - held)
-            await_bytes(self.buffer.at[region], self.recv_sems.at[step])
+            await_bytes(self.buffer.at[region], self.recv_sems.at[step - self.skipped])
 
     class Scatter:
         def __init__(self, kept, out_buffer, in_buffer, send_sem, recv_sems, plans, spans):
@@ -362,14 +363,11 @@
         plans, back_spans,
     )
     gathers = [
-        Gather(hidden.at[chunk, :, :, columns[chunk]], send_sem.at[2], all_recv_sem.at[chunk])
+        Gather(hidden.at[chunk, :, :, columns[chunk]], send_sem.at[2], all_recv_sem.at[chunk], 1)
         for chunk in range(CHUNKS)
     ]
-    route = Gather(routing, send_sem.at[3], route_recv_sem)
-
-    pl.semaphore_wait(barrier, len(friends))
-    share(0)
-    share(1)
+    route = Gather(routing, send_sem.at[3], route_recv_sem, 0)
+
     for chunk in range(CHUNKS):
         out_loads[chunk].wait()
         projected = jnp.dot(
@@ -377,6 +375,10 @@
             w_out[:, spans[chunk]],
             preferred_element_type=jnp.float32,
         )
+        if chunk == 0:
+            pl.semaphore_wait(barrier, len(friends))
+            share(0)
+            share(1)
         first_sum.start(
             chunk, 0, lambda place: projected[place * rows : (place + 1) * rows]
         )
@@ -606,7 +608,7 @@
             dma((11 + CHUNKS,)),
             dma((4,)),
             dma((CHUNKS, 2)),
-            dma((CHUNKS, len(groups))),
+            dma((CHUNKS, len(groups) - 1)),
             dma((len(groups),)),
             dma((len(BACK), len(groups))),
             dma((3,)),

time: 33.5 us -> 33.4 us (level)
  no operation moved by 1% of the time
where the time goes in v4:
time: 33.4 us; the launch traced here: 33.2 us
  Pallas kernels  32.6 us (98%)
  local copies, waits for them, and re-layouts  0.63 us (2%)
    pallas_call x1, Pallas kernels, body(): pl.pallas_call(functools.partial(layer_kernel, count), out_shape=pltpu.VM...  32.6 us

profile of v4, /device:TPU:0, one launch (start us, length us, event | category | flops | bytes accessed | tf_op | source)
XLA Modules:
  0.0 33.2 jit_solution(14042335323731776315)
XLA Ops:
  0.0 32.6 %shard_map.118 = bf16[16,2048]{1,0:T(8,128)(2,1)S(1)} custom-call(s32[4,4]{1,0:T(4,128)} %block_table_in.1, s32[1,4]{1,0:T(1,128)} %cache_lengths_in.1, bf16[128,512]{1,0:T(8,128)(2,1)} %queries_in.1, bf16[2,128,128]{2,1,0:T(8,128)(2,1)} %tree_in.1, bf16[2,16,32,128]{3,2,1,0:T(8,128)(2,1)} %cache_in.1, s32[4,32]{1,0:T(4,128)} %parents_in.1, ...), custom_call_target="tpu_custom_call" | custom-call | tf_op jit(solution)/shard_map/pallas_call | solution.py:577
  32.6 0.6 %copy.14 = bf16[16,2048]{1,0:T(8,128)(2,1)} copy(bf16[16,2048]{1,0:T(8,128)(2,1)S(1)} %shard_map.118) | data formatting | bytes 131072

commit v5 on v4

--- a/solution.py
+++ b/solution.py
@@ -7,7 +7,7 @@
 from jax.experimental.pallas import tpu as pltpu
 from jax.sharding import PartitionSpec as P
 
-FRONT = (3, 5, 5, 3)
+FRONT = (2, 4, 4, 4, 2)
 BACK = (4, 4, 4, 4)
 DIRECT = 2
 CHUNKS = len(FRONT)

time: 33.4 us -> 33.5 us (level)
  no operation moved by 1% of the time
where the time goes in v5:
time: 33.5 us; the launch traced here: 33.3 us
  Pallas kernels  32.7 us (98%)
  local copies, waits for them, and re-layouts  0.63 us (2%)
    pallas_call x1, Pallas kernels, body(): pl.pallas_call(functools.partial(layer_kernel, count), out_shape=pltpu.VM...  32.7 us

profile of v5, /device:TPU:0, one launch (start us, length us, event | category | flops | bytes accessed | tf_op | source)
XLA Modules:
  0.0 33.3 jit_solution(15413729547514226503)
XLA Ops:
  0.0 32.7 %shard_map.118 = bf16[16,2048]{1,0:T(8,128)(2,1)S(1)} custom-call(s32[4,4]{1,0:T(4,128)} %block_table_in.1, s32[1,4]{1,0:T(1,128)} %cache_lengths_in.1, bf16[128,512]{1,0:T(8,128)(2,1)} %queries_in.1, bf16[2,128,128]{2,1,0:T(8,128)(2,1)} %tree_in.1, bf16[2,16,32,128]{3,2,1,0:T(8,128)(2,1)} %cache_in.1, s32[4,32]{1,0:T(4,128)} %parents_in.1, ...), custom_call_target="tpu_custom_call" | custom-call | tf_op jit(solution)/shard_map/pallas_call | solution.py:577
  32.7 0.6 %copy.14 = bf16[16,2048]{1,0:T(8,128)(2,1)} copy(bf16[16,2048]{1,0:T(8,128)(2,1)S(1)} %shard_map.118) | data formatting | bytes 131072
